TPU v7x, 32 devices: a whole 2x2x4 slice. The times are simulated.
32 devices in a mesh: pairs: 2 (over y), blk: 8 (over z, x), panel: 2 (over core).
Axes of the slice: x: 2, y: 2, z: 4, core: 2. Of those that a mesh axis runs over, the one named last changes fastest.
Arguments:
- first_frame: bfloat16 [4096, 256], P(('pairs', 'blk', 'panel')), parts along dimension 0, may hold values from -8 to 8
- second_frame: bfloat16 [16, 8, 16, 256], P(('pairs', 'blk'), None, 'panel'), parts along dimension 0, may hold values from -8 to 8
Outputs:
- matched: float32 [4, 2, 4096], P(None, None, ('pairs', 'blk', 'panel')), parts along dimension 2
- energy: float32 [4, 4096], P(None, ('pairs', 'blk', 'panel')), parts along dimension 1
There are 2 independent parts, one for each index of `pairs`. A program takes and returns all parts, laid end to end along the dimension named above; each array names one. Nothing has to cross between parts.
All inputs are finite; a program needn't handle non-finite values.
Results may differ from a plain program's by a relative error of at most 0.014.
Values may be sent and summed in bfloat16 or wider, within the bound.
A program may use at most 128 MiB of HBM per device.

v0:
```python
import math

import jax
import jax.numpy as jnp
from jax import lax
from jax.sharding import PartitionSpec as P

LEVELS = 4
COLBLK = 8
BCOLS = 16


neg_large = -1e30


def build_levels(tile_batch):
    result = [tile_batch]
    pooled = tile_batch.astype(jnp.float32)
    for level_index in range(1, LEVELS):
        tile_count, height, columns, channels = pooled.shape
        pooled = pooled.reshape(tile_count, height // 2, 2, columns // 2, 2, channels).mean(
            axis=(2, 4)
        )
        result.append(pooled.astype(jnp.bfloat16))
    return result


def accumulate(carry_state, level_pieces, queries, col_start, total_rows, total_cols):
    maxima, totals = carry_state
    new_maxima = []
    new_totals = []
    for level_index in range(len(level_pieces)):
        level_piece = level_pieces[level_index]
        tile_count, height, columns, channels = level_piece.shape
        key_rows = level_piece.reshape(tile_count * height * columns, channels)
        factor = 3.0 * 2.0**level_index / math.sqrt(channels)
        scores = (
            jnp.einsum("kc,qc->kq", key_rows, queries, preferred_element_type=jnp.float32) * factor
        )
        merged_top = jnp.maximum(maxima[level_index], jnp.max(scores, axis=0))
        weights = jnp.exp(scores - merged_top[None, :])
        spacing = 2**level_index
        block_ids = jnp.arange(tile_count)
        row_index = (block_ids // COLBLK)[:, None, None] * height + jnp.arange(height)[
            None, :, None
        ]
        col_index = (
            (block_ids % COLBLK)[:, None, None] * (BCOLS // spacing)
            + col_start // spacing
            + jnp.arange(columns)[None, None, :]
        )
        row_grid = jnp.broadcast_to(row_index, (tile_count, height, columns)).astype(jnp.float32)
        col_grid = jnp.broadcast_to(col_index, (tile_count, height, columns)).astype(jnp.float32)
        row_pos = (row_grid + 0.5) * (float(spacing) / total_rows)
        col_pos = (col_grid + 0.5) * (float(spacing) / total_cols)
        unit_row = jnp.ones_like(row_pos)
        position_rows = jnp.stack([unit_row.reshape(-1), row_pos.reshape(-1), col_pos.reshape(-1)])
        block_totals = jnp.dot(
            position_rows,
            weights,
            precision=lax.Precision.HIGHEST,
            preferred_element_type=jnp.float32,
        )
        rescale = jnp.exp(maxima[level_index] - merged_top)
        new_totals.append(totals[level_index] * rescale[None, :] + block_totals)
        new_maxima.append(merged_top)
    return (jnp.stack(new_maxima), jnp.stack(new_totals))


def body(first_frame, second_frame):
    cycle_size = lax.axis_size("blk")
    panels = lax.axis_size("panel")
    block_count, tile_rows, tile_cols, channels = second_frame.shape
    total_rows = tile_rows * cycle_size // COLBLK
    total_cols = BCOLS * COLBLK
    col_start = lax.axis_index("panel") * tile_cols
    queries = lax.all_gather(first_frame, "panel", axis=0, tiled=True)
    query_count = queries.shape[0]
    init_state = (
        jnp.full((LEVELS, query_count), neg_large, jnp.float32),
        jnp.zeros((LEVELS, 3, query_count), jnp.float32),
    )
    level_zero, level_one, level_two, level_three = build_levels(second_frame)
    maxima, totals = accumulate(
        init_state,
        list(
            (
                lax.all_gather(level_zero, "blk", axis=0, tiled=True),
                lax.all_gather(level_one, "blk", axis=0, tiled=True),
                lax.all_gather(level_two, "blk", axis=0, tiled=True),
                lax.all_gather(level_three, "blk", axis=0, tiled=True),
            )
        ),
        queries,
        col_start,
        total_rows,
        total_cols,
    )
    half_count = query_count // panels
    own_max, own_tot = (
        lax.all_to_all(
            maxima.reshape(LEVELS, 1, panels, half_count),
            "panel",
            split_axis=2,
            concat_axis=2,
            tiled=True,
        ),
        lax.all_to_all(
            totals.reshape(LEVELS, 3, panels, half_count),
            "panel",
            split_axis=2,
            concat_axis=2,
            tiled=True,
        ),
    )
    merged = jnp.max(own_max, axis=2)
    totals = jnp.sum(own_tot * jnp.exp(own_max - merged[:, :, None, :]), axis=2)
    maxima = merged[:, 0, :]
    energy = maxima + jnp.log(totals[:, 0, :])
    matched = totals[:, 1:, :] / totals[:, 0:1, :]
    return (matched, energy)


def solution(mesh):
    placed = (P(("pairs", "blk", "panel"), None), P(("pairs", "blk"), None, "panel", None))
    return jax.shard_map(
        body,
        mesh=mesh,
        in_specs=placed,
        out_specs=(P(None, None, ("pairs", "blk", "panel")), P(None, ("pairs", "blk", "panel"))),
        check_vma=False,
    )
```

profile of v0, /device:TPU:0, one launch (start us, length us, event | category | flops | bytes accessed | tf_op | source)
XLA Modules:
  0.0 125.8 jit_solution(9972526232094171274)
XLA Ops:
  0.6 0.0 copy-start
  0.6 0.9 reshape.573
  1.5 0.0 copy-done
  1.5 0.0 copy-start.1
  1.5 32.7 %all_gather.15 = bf16[8,8,8,256]{3,2,1,0:T(8,128)(2,1)S(1)} all-gather(bf16[1,8,8,256]{3,2,1,0:T(8,128)(2,1)S(1)} %copy-done), channel_id=1, replica_groups=mesh['pairs'=2,'blk'=8,'panel'=2] {'blk'}, dimensions={0}, use_global_device_ids=true | all-gather | bytes 294912 | tf_op jit(solution)/shard_map/all_gather | solution.py:88
  34.2 0.0 copy-done.1
  34.2 1.9 %all_gather.16 = bf16[256,256]{1,0:T(8,128)(2,1)S(1)} all-gather(bf16[128,256]{1,0:T(8,128)(2,1)S(1)} %copy-done.1), channel_id=1, replica_groups=mesh['pairs'=2,'blk'=8,'panel'=2] {'panel'}, dimensions={0}, use_global_device_ids=true | all-gather | bytes 196608 | tf_op jit(solution)/shard_map/all_gather | solution.py:77
  36.1 0.1 reduce_sum.36
  36.2 30.5 %all-gather = bf16[32,4,256]{2,1,0:T(4,128)(2,1)S(1)} all-gather(bf16[4,4,256]{2,1,0:T(4,128)(2,1)S(1)} %get-tuple-element.6), channel_id=2, replica_groups=mesh['pairs'=2,'blk'=8,'panel'=2] {'blk'}, dimensions={0}, use_global_device_ids=true | all-gather | bytes 73728 | tf_op jit(solution)/shard_map/all_gather | solution.py:89
  66.7 0.2 fusion.48
  67.0 26.1 %all-gather.1 = bf16[16,2,256]{2,1,0:T(2,128)(2,1)S(1)} all-gather(bf16[2,2,256]{2,1,0:T(2,128)(2,1)S(1)} %get-tuple-element.8), channel_id=3, replica_groups=mesh['pairs'=2,'blk'=8,'panel'=2] {'blk'}, dimensions={0}, use_global_device_ids=true | all-gather | bytes 18432 | tf_op jit(solution)/shard_map/all_gather | solution.py:90
  93.2 0.2 fusion.47
  93.4 19.0 %all-gather.3 = bf16[8,1,256]{2,1,0:T(2,128)(2,1)S(1)} all-gather(bf16[1,1,256]{2,1,0:T(2,128)(2,1)S(1)} %reshape.580), channel_id=4, replica_groups=mesh['pairs'=2,'blk'=8,'panel'=2] {'blk'}, dimensions={0}, use_global_device_ids=true | all-gather | bytes 4608 | tf_op jit(solution)/shard_map/all_gather | solution.py:91
  112.4 0.2 fusion.46
  112.7 0.3 fusion.49
  113.0 0.6 pad_maximum_fusion.1
  113.6 3.2 %all-to-all-start.1 = ((f32[4,1,2,128]{3,0,1,2:T(4,128)}), f32[4,1,2,128]{3,0,1,2:T(4,128)S(1)}, u32[]{:S(2)}, u32[]{:S(2)}) async-start(f32[4,1,2,128]{3,0,1,2:T(4,128)} %pad_maximum_fusion.1), calls=%async_computation.1 | async-start | bytes 8192 | tf_op jit(solution)/shard_map/all_to_all | solution.py:101
  116.9 0.1 add_multiply_fusion.2
  117.0 0.1 mul.250
  117.1 0.1 add_multiply_fusion.3
  117.1 0.1 broadcast_in_dim.14
  117.2 0.1 mul.246
  117.4 0.2 convolution_add_fusion.2
  117.6 0.1 add_multiply_fusion
  117.7 0.1 mul.260
  117.8 0.1 add_multiply_fusion.1
  117.9 0.1 broadcast_in_dim.16
  118.0 0.1 mul.256
  118.1 0.2 convolution_add_fusion.1
  118.3 0.2 convolution_add_fusion
  118.5 0.1 add_multiply_fusion.4
  118.6 0.1 mul.239
  118.7 0.1 add_multiply_fusion.5
  118.8 0.1 broadcast_in_dim.12
  118.9 0.1 mul.234
  119.0 0.3 convolution_add_fusion.3
  119.3 0.1 stack.35
  119.4 0.6 pad_maximum_fusion
  120.0 0.0 all-to-all-done.1
  120.0 3.2 %all-to-all-start = ((f32[4,3,2,128]{3,0,1,2:T(4,128)}), f32[4,3,2,128]{3,0,1,2:T(4,128)S(1)}, u32[]{:S(2)}, u32[]{:S(2)}) async-start(f32[4,3,2,128]{3,0,1,2:T(4,128)} %pad_maximum_fusion), calls=%async_computation | async-start | bytes 24576 | tf_op jit(solution)/shard_map/all_to_all | solution.py:108
  123.3 1.3 %all-to-all-done = f32[4,3,2,128]{3,0,1,2:T(4,128)S(1)} async-done(((f32[4,3,2,128]{3,0,1,2:T(4,128)}), f32[4,3,2,128]{3,0,1,2:T(4,128)S(1)}, u32[]{:S(2)}, u32[]{:S(2)}) %all-to-all-start) | async-done | bytes 12320 | tf_op jit(solution)/shard_map/all_to_all | solution.py:108
  124.6 0.6 log_add_fusion
  125.2 0.6 copy_divide_fusion
  (35 shorter events, 0.3 us)
Async XLA Ops:
  0.6 0.9 copy-start
  1.5 32.7 %copy-start.1 = (bf16[128,256]{1,0:T(8,128)(2,1)S(1)}, bf16[128,256]{1,0:T(8,128)(2,1)}, u32[]{:S(2)}) copy-start(bf16[128,256]{1,0:T(8,128)(2,1)} %param.2) | copy-start | bytes 196612
  113.6 6.4 %all-to-all-start.1 = ((f32[4,1,2,128]{3,0,1,2:T(4,128)}), f32[4,1,2,128]{3,0,1,2:T(4,128)S(1)}, u32[]{:S(2)}, u32[]{:S(2)}) async-start(f32[4,1,2,128]{3,0,1,2:T(4,128)} %pad_maximum_fusion.1), calls=%async_computation.1 | async-start | bytes 8192 | tf_op jit(solution)/shard_map/all_to_all | solution.py:101
  120.0 4.6 %all-to-all-start = ((f32[4,3,2,128]{3,0,1,2:T(4,128)}), f32[4,3,2,128]{3,0,1,2:T(4,128)S(1)}, u32[]{:S(2)}, u32[]{:S(2)}) async-start(f32[4,3,2,128]{3,0,1,2:T(4,128)} %pad_maximum_fusion), calls=%async_computation | async-start | bytes 24576 | tf_op jit(solution)/shard_map/all_to_all | solution.py:108
where the time goes:
time: 126 us
  blocking collectives  110 us (87%)
  starting transfers between devices  6.45 us (5%)
  other arithmetic  3.09 us (2%)
  local copies, waits for them, and re-layouts  1.92 us (2%)
  matrix products  1.83 us (1%)
  waiting for transfers between devices  1.33 us (1%)
    all_gather x1, blocking collectives, body(): lax.all_gather(level_zero, 'blk', axis=0, tiled=True)  32.7 us
    all_gather x1, blocking collectives, body(): lax.all_gather(level_one, 'blk', axis=0, tiled=True)  30.5 us
    all_gather x1, blocking collectives, body(): lax.all_gather(level_two, 'blk', axis=0, tiled=True)  26.1 us
    all_gather x1, blocking collectives, body(): lax.all_gather(level_three, 'blk', axis=0, tiled=True)  19 us
    all_to_all x1, starting transfers between devices, body(): lax.all_to_all(totals.reshape(LEVELS, 3, panels, half_count), 'panel', sp...  3.23 us
    all_to_all x1, starting transfers between devices, body(): lax.all_to_all(maxima.reshape(LEVELS, 1, panels, half_count), 'panel', sp...  3.22 us
  transfers between devices with their start and end apart: 2, of which 1 were waited for; matrix products, arithmetic and copies ran while one was open for 2% of the time, Pallas kernels for 0%

commit v1 on v0

v1 whole, which is shorter than its diff:
```python
import functools
import math

import jax
import jax.numpy as jnp
from jax import lax
from jax.experimental import pallas as pl
from jax.experimental.pallas import tpu as pltpu
from jax.sharding import PartitionSpec as P

LEVELS = 4
COLBLK = 8
BCOLS = 16
NEG = -1e30
MESH = pl.DeviceIdType.MESH


def inner_size(blk):
    inner = 1
    while blk % (inner * 2) == 0 and (inner * 2) ** 2 * 2 <= blk:
        inner *= 2
    return inner


def partials(scores, sources, rows, cols, total_rows, total_cols):
    n = len(sources)
    q = scores.shape[-1]
    col = lax.broadcasted_iota(jnp.int32, (cols, q), 0)
    tops, totals, row_sums, col_sums = [], [], [], []
    pooled = scores.reshape(n, rows, cols, q)
    for level in range(LEVELS):
        step = 2**level
        if level:
            height = rows // step
            pairs = pooled.reshape(n, height, 2, cols, q)
            pooled = pairs[:, :, 0] + pairs[:, :, 1]
            pooled = pooled + pltpu.roll(pooled, step // 2, 2)
            pooled = 0.5 * pooled
            valid = (col & (step - 1)) == step - 1
            values = jnp.where(valid[None, None], pooled, NEG)
        else:
            height = rows
            values = pooled
        top = jnp.max(jnp.max(values, axis=(0, 1)), axis=0, keepdims=True)
        weights = jnp.exp(values - top)
        col_in = ((col >> level).astype(jnp.float32) + 0.5) * (step / total_cols)
        total = row_sum = col_sum = None
        for s, (row_base, col_base) in enumerate(sources):
            part = weights[s, 0]
            part_row = weights[s, 0] * (0.5 * step / total_rows)
            for i in range(1, height):
                part = part + weights[s, i]
                part_row = part_row + weights[s, i] * ((i + 0.5) * step / total_rows)
            part_row = part_row + part * row_base
            part_col = part * (col_in + col_base)
            total = part if total is None else total + part
            row_sum = part_row if row_sum is None else row_sum + part_row
            col_sum = part_col if col_sum is None else col_sum + part_col
        tops.append(top)
        totals.append(jnp.sum(total, axis=0, keepdims=True))
        row_sums.append(jnp.sum(row_sum, axis=0, keepdims=True))
        col_sums.append(jnp.sum(col_sum, axis=0, keepdims=True))
    return tops + totals + row_sums + col_sums


def kernel(dims, q_ref, k_ref, matched_ref, energy_ref, qbuf, kbuf, sent, got, local_sem,
           k_send, k_recv, q_send, q_recv, p_send, p_recv):
    blk, panels, inner, rows, cols = dims
    outer, group = blk // inner, inner * panels
    keys = rows * cols
    total_rows, total_cols = rows * blk // COLBLK, BCOLS * COLBLK
    me_blk, me_panel = lax.axis_index("blk"), lax.axis_index("panel")
    me_outer, me_inner = me_blk // inner, me_blk % inner
    me_group = me_inner * panels + me_panel

    def line_id(shift):
        there = lax.rem(me_outer + shift + outer, outer)
        return {"blk": there * inner + me_inner, "panel": me_panel}

    def group_id(shift):
        there = lax.rem(me_group + shift + group, group)
        return {"blk": me_outer * inner + there // panels, "panel": there % panels}

    barrier = pltpu.get_barrier_semaphore()
    for d in range(1, outer):
        pl.semaphore_signal(barrier, inc=1, device_id=line_id(d), device_id_type=MESH)
    for d in range(1, group):
        pl.semaphore_signal(barrier, inc=1, device_id=group_id(d), device_id_type=MESH)
    own_k = pltpu.make_async_copy(k_ref, kbuf.at[0], local_sem.at[0])
    own_q = pltpu.make_async_copy(q_ref, qbuf.at[0], local_sem.at[1])
    own_k.start()
    own_q.start()
    own_k.wait()
    own_q.wait()
    pl.semaphore_wait(barrier, outer + group - 2)

    key_copies, query_copies = {}, {}
    for d in range(1, outer):
        key_copies[d] = pltpu.make_async_remote_copy(
            kbuf.at[0], kbuf.at[d], k_send.at[d - 1], k_recv.at[d - 1],
            device_id=line_id(d), device_id_type=MESH)
        key_copies[d].start()
    for d in range(1, group):
        query_copies[d] = pltpu.make_async_remote_copy(
            qbuf.at[0], qbuf.at[d], q_send.at[d - 1], q_recv.at[d - 1],
            device_id=group_id(d), device_id_type=MESH)
        query_copies[d].start()

    sources = []
    for d in range(outer):
        block = lax.rem(me_outer - d + outer, outer) * inner + me_inner
        row_base = (block // COLBLK).astype(jnp.float32) * (rows / total_rows)
        col_base = ((block % COLBLK) * BCOLS + me_panel * cols).astype(jnp.float32) * (1.0 / total_cols)
        sources.append((row_base, col_base))

    for d in range(1, outer):
        key_copies[d].wait_recv()
    all_keys = kbuf[...].reshape(outer * keys, kbuf.shape[-1])
    factor = 3.0 / math.sqrt(kbuf.shape[-1])

    def score(d):
        raw = lax.dot_general(all_keys, qbuf[d], (((1,), (1,)), ((), ())),
                              preferred_element_type=jnp.float32)
        rows_out = partials(raw * factor, sources, rows, cols, total_rows, total_cols)
        sent[d] = jnp.concatenate(rows_out, axis=0)

    back = {}
    for d in range(1, group):
        query_copies[d].wait_recv()
        score(d)
        back[d] = pltpu.make_async_remote_copy(
            sent.at[d], got.at[d], p_send.at[d - 1], p_recv.at[d - 1],
            device_id=group_id(-d), device_id_type=MESH)
        back[d].start()
    score(0)
    parts = [sent[0]]
    for d in range(1, group):
        back[d].wait_recv()
        parts.append(got[d])
    top = functools.reduce(jnp.maximum, [p[:LEVELS] for p in parts])
    sums = None
    for p in parts:
        scale = jnp.exp(p[:LEVELS] - top)
        term = [p[LEVELS * i : LEVELS * (i + 1)] * scale for i in (1, 2, 3)]
        sums = term if sums is None else [a + b for a, b in zip(sums, term)]
    total, row_sum, col_sum = sums
    energy_ref[...] = top + jnp.log(total)
    matched_ref[:, 0, :] = row_sum / total
    matched_ref[:, 1, :] = col_sum / total
    for copies in (key_copies, query_copies, back):
        for copy in copies.values():
            copy.wait_send()


def body(blk, panels, first_frame, second_frame):
    queries, channels = first_frame.shape
    _, rows, cols, _ = second_frame.shape
    inner = inner_size(blk)
    outer, group = blk // inner, inner * panels
    keys = second_frame.reshape(rows * cols, channels)
    dma = pltpu.SemaphoreType.DMA
    matched, energy = pl.pallas_call(
        functools.partial(kernel, (blk, panels, inner, rows, cols)),
        out_shape=(jax.ShapeDtypeStruct((LEVELS, 2, queries), jnp.float32),
                   jax.ShapeDtypeStruct((LEVELS, queries), jnp.float32)),
        in_specs=[pl.BlockSpec(memory_space=pl.ANY)] * 2,
        out_specs=(pl.BlockSpec(memory_space=pltpu.VMEM), pl.BlockSpec(memory_space=pltpu.VMEM)),
        scratch_shapes=[
            pltpu.VMEM((group, queries, channels), jnp.bfloat16),
            pltpu.VMEM((outer, rows * cols, channels), jnp.bfloat16),
            pltpu.VMEM((group, 4 * LEVELS, queries), jnp.float32),
            pltpu.VMEM((group, 4 * LEVELS, queries), jnp.float32),
            dma((2,)),
            dma((outer - 1,)), dma((outer - 1,)),
            dma((group - 1,)), dma((group - 1,)),
            dma((group - 1,)), dma((group - 1,)),
        ],
        compiler_params=pltpu.CompilerParams(collective_id=0, has_side_effects=True),
        name="corr",
    )(first_frame, keys)
    return matched, energy


def solution(mesh):
    placed = (P(("pairs", "blk", "panel"), None), P(("pairs", "blk"), None, "panel", None))
    return jax.shard_map(
        functools.partial(body, mesh.shape["blk"], mesh.shape["panel"]),
        mesh=mesh,
        in_specs=placed,
        out_specs=(P(None, None, ("pairs", "blk", "panel")), P(None, ("pairs", "blk", "panel"))),
        check_vma=False,
    )
```

time: 126 us -> 15.8 us (0.13)
  blocking collectives: 110 us -> 0 us
  Pallas kernels: 0 us -> 13.1 us
  starting transfers between devices: 6.45 us -> 0 us
  other arithmetic: 3.09 us -> 0 us
  matrix products: 1.83 us -> 0 us
  waiting for transfers between devices: 1.33 us -> 0 us
    all_gather x5 -> x0, blocking collectives: 110 us -> none  [the longest x1 32.7 us: body(): lax.all_gather(level_zero, 'blk', axis=0, tiled=True)]
    pallas_call x0 -> x1, Pallas kernels: none -> 13.1 us  [body(): pl.pallas_call(functools.partial(kernel, (blk, panels, inner, rows, cols)...]
    all_to_all x2 -> x0, starting transfers between devices: 6.45 us -> none  [the longest x1 3.23 us: body(): lax.all_to_all(totals.reshape(LEVELS, 3, panels, half_count), 'panel', sp...]
    unnamed x5 -> x4, local copies, waits for them, and re-layouts: 0.02 us -> 1.85 us
    dot_general x8 -> x0, matrix products: 1.83 us -> none  [the longest x4 0.93 us: accumulate(): jnp.dot(position_rows, weights, precision=lax.Precision.HIGHEST, preferre...]
    all_to_all x2 -> x0, waiting for transfers between devices: 1.33 us -> none  [the longest x1 1.33 us: body(): lax.all_to_all(totals.reshape(LEVELS, 3, panels, half_count), 'panel', sp...]
  transfers between devices with their start and end apart: 2 -> 0, of which waited for: 1 -> 0; matrix products, arithmetic and copies ran while one was open for 2% -> 0% of each run, Pallas kernels for 0% -> 0%
where the time goes in v1:
time: 15.8 us; the launch traced here: 15.6 us
  Pallas kernels  13.1 us (83%)
  local copies, waits for them, and re-layouts  1.85 us (12%)
  between operations  0.65 us (4%)
    pallas_call x1, Pallas kernels, body(): pl.pallas_call(functools.partial(kernel, (blk, panels, inner, rows, cols)...  13.1 us
    unnamed x4, local copies, waits for them, and re-layouts  1.85 us

profile of v1, /device:TPU:0, one launch (start us, length us, event | category | flops | bytes accessed | tf_op | source)
XLA Modules:
  0.0 15.6 jit_solution(7252921258421892281)
XLA Ops:
  0.6 13.1 %corr.1 = (f32[4,2,128]{2,1,0:T(2,128)}, f32[4,128]{1,0:T(4,128)}) custom-call(bf16[128,256]{1,0:T(8,128)(2,1)} %q_ref.1, bf16[64,256]{1,0:T(8,128)(2,1)} %bitcast.1), custom_call_target="tpu_custom_call" | custom-call | tf_op jit(solution)/shard_map/corr/pallas_call | solution.py:162
  13.8 0.0 copy-start
  13.8 1.3 %copy.6 = f32[4,2,128]{2,1,0:T(2,128)} copy(f32[4,2,128]{2,1,0:T(2,128)} %get-tuple-element.4) | data formatting | bytes 8192
  15.0 0.0 copy-done
  15.0 0.6 %copy.7 = f32[4,128]{1,0:T(4,128)} copy(f32[4,128]{1,0:T(4,128)S(1)} %copy-done) | data formatting | bytes 4096
Async XLA Ops:
  13.8 1.3 %copy-start = (f32[4,128]{1,0:T(4,128)S(1)}, f32[4,128]{1,0:T(4,128)}, u32[]{:S(2)}) copy-start(f32[4,128]{1,0:T(4,128)} %get-tuple-element.5) | copy-start | bytes 6148

commit v2 on v1

--- a/solution.py
+++ b/solution.py
@@ -63,7 +63,7 @@
     return tops + totals + row_sums + col_sums
 
 
-def kernel(dims, q_ref, k_ref, matched_ref, energy_ref, qbuf, kbuf, sent, got, local_sem,
+def kernel(dims, q_ref, k_ref, merged_ref, qbuf, kbuf, sent, got, local_sem,
            k_send, k_recv, q_send, q_recv, p_send, p_recv):
     blk, panels, inner, rows, cols = dims
     outer, group = blk // inner, inner * panels
@@ -144,12 +144,17 @@
         term = [p[LEVELS * i : LEVELS * (i + 1)] * scale for i in (1, 2, 3)]
         sums = term if sums is None else [a + b for a, b in zip(sums, term)]
     total, row_sum, col_sum = sums
-    energy_ref[...] = top + jnp.log(total)
-    matched_ref[:, 0, :] = row_sum / total
-    matched_ref[:, 1, :] = col_sum / total
+    merged_ref[...] = jnp.concatenate([top, total, row_sum, col_sum], axis=0)
     for copies in (key_copies, query_copies, back):
         for copy in copies.values():
             copy.wait_send()
+
+
+def finish(merged_ref, matched_ref, energy_ref):
+    top, total = merged_ref[:LEVELS], merged_ref[LEVELS : 2 * LEVELS]
+    energy_ref[...] = top + jnp.log(total)
+    matched_ref[:, 0, :] = merged_ref[2 * LEVELS : 3 * LEVELS] / total
+    matched_ref[:, 1, :] = merged_ref[3 * LEVELS :] / total
 
 
 def body(blk, panels, first_frame, second_frame):
@@ -159,12 +164,11 @@
     outer, group = blk // inner, inner * panels
     keys = second_frame.reshape(rows * cols, channels)
     dma = pltpu.SemaphoreType.DMA
-    matched, energy = pl.pallas_call(
+    merged = pl.pallas_call(
         functools.partial(kernel, (blk, panels, inner, rows, cols)),
-        out_shape=(jax.ShapeDtypeStruct((LEVELS, 2, queries), jnp.float32),
-                   jax.ShapeDtypeStruct((LEVELS, queries), jnp.float32)),
+        out_shape=jax.ShapeDtypeStruct((4 * LEVELS, queries), jnp.float32),
         in_specs=[pl.BlockSpec(memory_space=pl.ANY)] * 2,
-        out_specs=(pl.BlockSpec(memory_space=pltpu.VMEM), pl.BlockSpec(memory_space=pltpu.VMEM)),
+        out_specs=pl.BlockSpec(memory_space=pltpu.VMEM),
         scratch_shapes=[
             pltpu.VMEM((group, queries, channels), jnp.bfloat16),
             pltpu.VMEM((outer, rows * cols, channels), jnp.bfloat16),
@@ -178,7 +182,14 @@
         compiler_params=pltpu.CompilerParams(collective_id=0, has_side_effects=True),
         name="corr",
     )(first_frame, keys)
-    return matched, energy
+    return pl.pallas_call(
+        finish,
+        out_shape=(jax.ShapeDtypeStruct((LEVELS, 2, queries), jnp.float32),
+                   jax.ShapeDtypeStruct((LEVELS, queries), jnp.float32)),
+        in_specs=[pl.BlockSpec(memory_space=pltpu.VMEM)],
+        out_specs=(pl.BlockSpec(memory_space=pltpu.VMEM), pl.BlockSpec(memory_space=pltpu.VMEM)),
+        name="finish",
+    )(merged)
 
 
 def solution(mesh):

time: 15.8 us -> 15.3 us (0.968)
  local copies, waits for them, and re-layouts: 1.85 us -> 0 us
  Pallas kernels: 13.1 us -> 14.4 us
    unnamed x4 -> x0, local copies, waits for them, and re-layouts: 1.85 us -> none
    pallas_call x0 -> x1, Pallas kernels: none -> 1.3 us  [body(): pl.pallas_call(finish, out_shape=(jax.ShapeDtypeStruct((LEVELS, 2, querie...]
where the time goes in v2:
time: 15.3 us; the launch traced here: 15.1 us
  Pallas kernels  14.4 us (94%)
  between operations  0.64 us (4%)
    pallas_call x1, Pallas kernels, body(): pl.pallas_call(functools.partial(kernel, (blk, panels, inner, rows, cols)...  13.1 us
    pallas_call x1, Pallas kernels, body(): pl.pallas_call(finish, out_shape=(jax.ShapeDtypeStruct((LEVELS, 2, querie...  1.3 us

profile of v2, /device:TPU:0, one launch (start us, length us, event | category | flops | bytes accessed | tf_op | source)
XLA Modules:
  0.0 15.1 jit_solution(3339385986351308710)
XLA Ops:
  0.6 13.1 %corr.1.merged_ref = f32[16,128]{1,0:T(8,128)} custom-call(bf16[128,256]{1,0:T(8,128)(2,1)} %q_ref.1, bf16[64,256]{1,0:T(8,128)(2,1)} %bitcast.1), custom_call_target="tpu_custom_call" | custom-call | tf_op jit(solution)/shard_map/corr/pallas_call | solution.py:167
  13.8 1.3 %finish.1 = (f32[4,2,128]{2,1,0:T(2,128)}, f32[4,128]{1,0:T(4,128)}) custom-call(f32[16,128]{1,0:T(8,128)} %corr.1.merged_ref), custom_call_target="tpu_custom_call" | custom-call | tf_op jit(solution)/shard_map/finish/pallas_call | solution.py:185

commit v3 on v2

--- a/solution.py
+++ b/solution.py
@@ -166,7 +166,7 @@
     dma = pltpu.SemaphoreType.DMA
     merged = pl.pallas_call(
         functools.partial(kernel, (blk, panels, inner, rows, cols)),
-        out_shape=jax.ShapeDtypeStruct((4 * LEVELS, queries), jnp.float32),
+        out_shape=pltpu.VMEM((4 * LEVELS, queries), jnp.float32),
         in_specs=[pl.BlockSpec(memory_space=pl.ANY)] * 2,
         out_specs=pl.BlockSpec(memory_space=pltpu.VMEM),
         scratch_shapes=[
@@ -189,7 +189,7 @@
         in_specs=[pl.BlockSpec(memory_space=pltpu.VMEM)],
         out_specs=(pl.BlockSpec(memory_space=pltpu.VMEM), pl.BlockSpec(memory_space=pltpu.VMEM)),
         name="finish",
-    )(merged)
+    )(pltpu.with_memory_space_constraint(merged, pltpu.VMEM))
 
 
 def solution(mesh):

time: 15.3 us -> 13.9 us (0.908)
  Pallas kernels: 14.4 us -> 13.1 us
    pallas_call x1, Pallas kernels: 1.3 us -> 0.61 us  [body(): pl.pallas_call(finish, out_shape=(jax.ShapeDtypeStruct((LEVELS, 2, querie...]
    pallas_call x1, Pallas kernels: 13.1 us -> 12.5 us  [body(): pl.pallas_call(functools.partial(kernel, (blk, panels, inner, rows, cols)...]
where the time goes in v3:
time: 13.9 us; the launch traced here: 13.8 us
  Pallas kernels  13.1 us (94%)
  between operations  0.64 us (5%)
    pallas_call x1, Pallas kernels, body(): pl.pallas_call(functools.partial(kernel, (blk, panels, inner, rows, cols)...  12.5 us
    pallas_call x1, Pallas kernels, body(): pl.pallas_call(finish, out_shape=(jax.ShapeDtypeStruct((LEVELS, 2, querie...  0.61 us

profile of v3, /device:TPU:0, one launch (start us, length us, event | category | flops | bytes accessed | tf_op | source)
XLA Modules:
  0.0 13.8 jit_solution(7974234743267785667)
XLA Ops:
  0.6 12.5 %corr.1.merged_ref = f32[16,128]{1,0:T(8,128)S(1)} custom-call(bf16[128,256]{1,0:T(8,128)(2,1)} %q_ref.1, bf16[64,256]{1,0:T(8,128)(2,1)} %bitcast.1), custom_call_target="tpu_custom_call" | custom-call | tf_op jit(solution)/shard_map/corr/pallas_call | solution.py:167
  13.2 0.6 %finish.1 = (f32[4,2,128]{2,1,0:T(2,128)}, f32[4,128]{1,0:T(4,128)}) custom-call(f32[16,128]{1,0:T(8,128)S(1)} %corr.1.merged_ref), custom_call_target="tpu_custom_call" | custom-call | tf_op jit(solution)/shard_map/finish/pallas_call | solution.py:185

commit v4 on v3

--- a/solution.py
+++ b/solution.py
@@ -71,21 +71,21 @@
     total_rows, total_cols = rows * blk // COLBLK, BCOLS * COLBLK
     me_blk, me_panel = lax.axis_index("blk"), lax.axis_index("panel")
     me_outer, me_inner = me_blk // inner, me_blk % inner
-    me_group = me_inner * panels + me_panel
 
     def line_id(shift):
         there = lax.rem(me_outer + shift + outer, outer)
         return {"blk": there * inner + me_inner, "panel": me_panel}
 
-    def group_id(shift):
-        there = lax.rem(me_group + shift + group, group)
-        return {"blk": me_outer * inner + there // panels, "panel": there % panels}
+    def slot_id(slot, sign=1):
+        there = lax.rem(me_inner + sign * (slot // panels) + inner, inner)
+        side = lax.rem(me_panel + sign * (slot % panels) + panels, panels)
+        return {"blk": me_outer * inner + there, "panel": side}
 
     barrier = pltpu.get_barrier_semaphore()
     for d in range(1, outer):
         pl.semaphore_signal(barrier, inc=1, device_id=line_id(d), device_id_type=MESH)
     for d in range(1, group):
-        pl.semaphore_signal(barrier, inc=1, device_id=group_id(d), device_id_type=MESH)
+        pl.semaphore_signal(barrier, inc=1, device_id=slot_id(d), device_id_type=MESH)
     own_k = pltpu.make_async_copy(k_ref, kbuf.at[0], local_sem.at[0])
     own_q = pltpu.make_async_copy(q_ref, qbuf.at[0], local_sem.at[1])
     own_k.start()
@@ -103,7 +103,7 @@
     for d in range(1, group):
         query_copies[d] = pltpu.make_async_remote_copy(
             qbuf.at[0], qbuf.at[d], q_send.at[d - 1], q_recv.at[d - 1],
-            device_id=group_id(d), device_id_type=MESH)
+            device_id=slot_id(d), device_id_type=MESH)
         query_copies[d].start()
 
     sources = []
@@ -125,12 +125,12 @@
         sent[d] = jnp.concatenate(rows_out, axis=0)
 
     back = {}
-    for d in range(1, group):
+    for d in sorted(range(1, group), key=lambda d: d < panels):
         query_copies[d].wait_recv()
         score(d)
         back[d] = pltpu.make_async_remote_copy(
             sent.at[d], got.at[d], p_send.at[d - 1], p_recv.at[d - 1],
-            device_id=group_id(-d), device_id_type=MESH)
+            device_id=slot_id(d, -1), device_id_type=MESH)
         back[d].start()
     score(0)
     parts = [sent[0]]

time: 13.9 us -> 13.6 us (0.978)
  Pallas kernels: 13.1 us -> 12.8 us
    pallas_call x1, Pallas kernels: 12.5 us -> 12.2 us  [body(): pl.pallas_call(functools.partial(kernel, (blk, panels, inner, rows, cols)...]
where the time goes in v4:
time: 13.6 us; the launch traced here: 13.5 us
  Pallas kernels  12.8 us (94%)
  between operations  0.64 us (5%)
    pallas_call x1, Pallas kernels, body(): pl.pallas_call(functools.partial(kernel, (blk, panels, inner, rows, cols)...  12.2 us
    pallas_call x1, Pallas kernels, body(): pl.pallas_call(finish, out_shape=(jax.ShapeDtypeStruct((LEVELS, 2, querie...  0.61 us

profile of v4, /device:TPU:0, one launch (start us, length us, event | category | flops | bytes accessed | tf_op | source)
XLA Modules:
  0.0 13.5 jit_solution(4046461481083573097)
XLA Ops:
  0.6 12.2 %corr.1.merged_ref = f32[16,128]{1,0:T(8,128)S(1)} custom-call(bf16[128,256]{1,0:T(8,128)(2,1)} %q_ref.1, bf16[64,256]{1,0:T(8,128)(2,1)} %bitcast.1), custom_call_target="tpu_custom_call" | custom-call | tf_op jit(solution)/shard_map/corr/pallas_call | solution.py:167
  12.9 0.6 %finish.1 = (f32[4,2,128]{2,1,0:T(2,128)}, f32[4,128]{1,0:T(4,128)}) custom-call(f32[16,128]{1,0:T(8,128)S(1)} %corr.1.merged_ref), custom_call_target="tpu_custom_call" | custom-call | tf_op jit(solution)/shard_map/finish/pallas_call | solution.py:185
